TPU v7x, 32 devices: a whole 2x2x4 slice. The times are simulated.
32 devices in a mesh: ctx: 16 (over z, x, core), dp: 2 (over y).
Axes of the slice: x: 2, y: 2, z: 4, core: 2. Of those that a mesh axis runs over, the one named last changes fastest.
Arguments:
- queries: bfloat16 [4096, 4096], P(None, ('ctx', 'dp')), may hold values from -6 to 6
- key_stream: bfloat16 [4096, 4096], P(None, ('ctx', 'dp')), may hold values from -6 to 6
- value_stream: bfloat16 [4096, 4096], P(None, ('ctx', 'dp')), may hold values from -6 to 6
- filters: float32 [256, 4096], P(('ctx', 'dp')), may hold values from -1 to 1
- bias: float32 [4096], P(('ctx', 'dp')), may hold values from -4 to 4
- grad_out: bfloat16 [4096, 4096], P(None, ('ctx', 'dp')), may hold values from -6 to 6
Outputs:
- out: bfloat16 [4096, 4096], P(None, ('ctx', 'dp'))
- grad_queries: bfloat16 [4096, 4096], P(None, ('ctx', 'dp'))
- grad_keys: bfloat16 [4096, 4096], P(None, ('ctx', 'dp'))
- grad_values: bfloat16 [4096, 4096], P(None, ('ctx', 'dp'))
- grad_filters: float32 [256, 4096], P(('ctx', 'dp'))
- grad_bias: float32 [4096], P(('ctx', 'dp'))
All inputs are finite; a program needn't handle non-finite values.
Results may differ from a plain program's by a relative error of at most 0.006.
Values may be sent and summed in bfloat16 or wider, within the bound.
No kernel may reach another device: no remote copies, remote signals or barrier semaphores. Data moves between devices by JAX's collectives and lax.ppermute only.
A program may use at most 128 MiB of HBM per device.

v0:
```python
import functools

import jax
import jax.numpy as jnp
from jax import lax
from jax.experimental import pallas as pl
from jax.experimental.pallas import tpu as pltpu
from jax.sharding import Mesh, PartitionSpec as P


F32 = jnp.float32
BF16 = jnp.bfloat16
WIDTH = 128
WIDE = 2 * WIDTH
TIMES = (((1,), (0,)), ((), ()))
TIMES_T = (((1,), (1,)), ((), ()))
RING = ("ctx_low", "dp")
TAP_PARTS = 2
STEPS = 2
MANY = 4
SWEEP = 4
UNROLL = 16


def pick(role, cases):
    for case in (0, 1):
        pl.when(role == case)(functools.partial(cases, case))


def prepare_kernel(role, q, k, v, g, first, own):
    def main(case):
        product = (k[...].astype(F32) * v[...].astype(F32)).astype(BF16)
        weighted = (q[...].astype(F32) * g[...].astype(F32)).astype(BF16)
        x, y = (product, weighted) if case == 0 else (weighted, product)
        for part in (0, 1):
            first[:, part] = x[part]
            own[:, part] = y[part]

    pick(role[0], main)


def prepare(role, q, k, v, g, ranks):
    channels, tokens = q.shape
    per = channels // (2 * ranks)
    view = lambda a: a.reshape(2, ranks, per, tokens)
    step = ranks // STEPS
    spec = pl.BlockSpec((2, step, per, tokens), lambda h, r: (0, h, 0, 0))
    out_spec = pl.BlockSpec((step, 2, per, tokens), lambda h, r: (h, 0, 0, 0))
    return pl.pallas_call(
        prepare_kernel,
        out_shape=(jax.ShapeDtypeStruct((ranks, 2, per, tokens), BF16),) * 2,
        grid_spec=pltpu.PrefetchScalarGridSpec(
            num_scalar_prefetch=1,
            grid=(STEPS,),
            in_specs=[spec] * 4,
            out_specs=(out_spec,) * 2,
        ),
        name="prepare",
    )(role, view(q), view(k), view(v), view(g))


def finish_kernel(role, q, k, v, g, one, two, out, gq, gk, gv):
    def main(case):
        for part in (0, 1):
            first, second = one[:, part].astype(F32), two[:, part].astype(F32)
            mixed, back = (first, second) if case == 0 else (second, first)
            out[part] = (q[part].astype(F32) * mixed).astype(BF16)
            gq[part] = (g[part].astype(F32) * mixed).astype(BF16)
            gk[part] = (back * v[part].astype(F32)).astype(BF16)
            gv[part] = (back * k[part].astype(F32)).astype(BF16)

    pick(role[0], main)


def finish(role, q, k, v, g, one, two, ranks):
    channels, tokens = q.shape
    per = channels // (2 * ranks)
    view = lambda a: a.reshape(2, ranks, per, tokens)
    step = ranks // STEPS
    spec = pl.BlockSpec((2, step, per, tokens), lambda h, r: (0, h, 0, 0))
    outs = pl.pallas_call(
        finish_kernel,
        out_shape=(jax.ShapeDtypeStruct((2, ranks, per, tokens), BF16),) * 4,
        grid_spec=pltpu.PrefetchScalarGridSpec(
            num_scalar_prefetch=1,
            grid=(STEPS,),
            in_specs=[spec] * 4
            + [pl.BlockSpec((step, 2, per, tokens), lambda h, r: (h, 0, 0, 0))] * 2,
            out_specs=(spec,) * 4,
        ),
        name="finish",
    )(role, view(q), view(k), view(v), view(g), one, two)
    return [o.reshape(channels, tokens) for o in outs]


def sweep(count, body):
    lax.fori_loop(0, count, lambda n, none: (body(n), none)[1], 0, unroll=min(count, SWEEP))


def build_band(line_of, tiles, case, lags):
    total = tiles[0].shape[1] // WIDTH - 1
    first = 0 if case == 0 else total - lags
    chunk = min(lags, 32)

    def step(c):
        c = c * chunk + first
        if isinstance(c, int):
            line = line_of(slice(c * WIDTH, (c + chunk + 1) * WIDTH))
        else:
            line = line_of(pl.ds(pl.multiple_of(c * WIDTH, WIDTH), (chunk + 1) * WIDTH))
        line = jnp.broadcast_to(line, (WIDTH, (chunk + 1) * WIDTH))
        band = pltpu.roll(line, 0, 1, stride=1, stride_axis=0)[:, WIDTH:]
        place = pl.ds(pl.multiple_of((c + 1) * WIDTH, WIDTH), chunk * WIDTH)
        top = band.astype(BF16)
        tiles[0][:, place] = top
        if len(tiles) > 1:
            tiles[1][:, place] = (band - top.astype(F32)).astype(BF16)

    if lags == chunk:
        step(0)
    else:
        lax.fori_loop(0, lags // chunk, lambda c, none: (step(c), none)[1], 0)


def square_of(tiles, case, d, turned):
    total = tiles.shape[1] // WIDTH - 1

    def tile(lag):
        if isinstance(d, int) and lag < 0:
            return jnp.zeros((WIDTH, WIDTH), BF16)
        at = lag + 1 if case == 0 else total - lag
        if isinstance(d, int):
            return tiles[:, at * WIDTH : (at + 1) * WIDTH]
        value = tiles[:, pl.ds(pl.multiple_of(jnp.clip(at, 0, total) * WIDTH, WIDTH), WIDTH)]
        return jnp.where(lag < 0, jnp.zeros_like(value), value)

    mid, less, more = tile(2 * d), tile(2 * d - 1), tile(2 * d + 1)
    if turned:
        less, more = more, less
    return jnp.concatenate(
        [jnp.concatenate([mid, more], axis=1), jnp.concatenate([less, mid], axis=1)], axis=0
    )


def dot(a, b, form=TIMES):
    return lax.dot_general(a, b, form, preferred_element_type=F32)


def gather_rows(case, src, dst, start, blocks, group):
    for i in range(blocks):
        at = i if case == 0 else blocks - 1 - i
        row = start + (i // 2) * group
        col = (i % 2) * WIDTH
        dst[row : row + group, col : col + WIDTH] = src[at]


def scatter_rows(case, value, dst, blocks, group):
    for i in range(blocks):
        at = i if case == 0 else blocks - 1 - i
        row = (i // 2) * group
        col = (i % 2) * WIDTH
        dst[at] = value[row : row + group, col : col + WIDTH].astype(BF16)


def apply_band(data, start, sign, shift, lags, tiles, case, turned, acc, group, base=None):
    rows = acc.shape[0]
    pairs = rows // group
    if pairs <= UNROLL:
        sums = [None] * pairs
        if base is not None:
            sums = [base[i * group : (i + 1) * group, :] for i in range(pairs)]
        for d in range(*lags):
            at = [i for i in range(pairs) if 0 <= i + sign * d + shift < pairs]
            low = start + (at[0] + sign * d + shift) * group
            block = data[low : low + len(at) * group, :]
            for part in tiles:
                found = dot(block, square_of(part, case, d, turned))
                for k, i in enumerate(at):
                    piece = found[k * group : (k + 1) * group]
                    sums[i] = piece if sums[i] is None else sums[i] + piece
        return jnp.concatenate(sums, axis=0)
    acc[...] = jnp.zeros_like(acc) if base is None else base[...]

    def step(d, none):
        low = pl.multiple_of(start + (sign * d + shift) * group, group)
        block = data[pl.ds(low, rows), :]
        for part in tiles:
            acc[...] += dot(block, square_of(part, case, d, turned))
        return none

    lax.fori_loop(*lags, step, 0)
    return acc[...]


def bias_term(data, bias, pairs, group):
    line = jnp.concatenate([bias, bias], axis=1)
    shaped = data.astype(F32).reshape(pairs, group, WIDE) * line[None]
    return shaped.reshape(pairs * group, WIDE)


def gather_line(case, src, dst, start, blocks, group):
    for i in range(blocks):
        at = i if case == 0 else blocks - 1 - i
        dst[start + i * group : start + (i + 1) * group, :] = src[at]


def flip_rows(data):
    down = lax.broadcasted_iota(jnp.int32, (WIDTH, WIDTH), 0)
    across = lax.broadcasted_iota(jnp.int32, (WIDTH, WIDTH), 1)
    mirror = jnp.where(down + across == WIDTH - 1, 1.0, 0.0).astype(BF16)
    return dot(mirror, data, TIMES_T).astype(BF16)


def correlate(case, turned, data, start, shift, lags, total, lines, group):
    rows = turned.shape[1]
    inside = lax.broadcasted_iota(jnp.int32, (WIDTH, WIDTH), 1) <= lax.broadcasted_iota(
        jnp.int32, (WIDTH, WIDTH), 0
    )

    def step(lag):
        low = start + (lag + shift) * group
        if not isinstance(lag, int):
            low = pl.multiple_of(low, group)
        square = dot(turned, data[pl.ds(low, rows), :])
        flat = pltpu.roll(square, 1, 1, stride=1, stride_axis=0)
        kept = jnp.where(inside, flat, 0.0)
        at = lag + 1 if case == 0 else total - lag
        kept = jnp.sum(kept.reshape(WIDTH // 8, 8, WIDTH), axis=0)
        lines[at] += kept
        lines[at - 1] += jnp.sum(flat.reshape(WIDTH // 8, 8, WIDTH), axis=0) - kept

    if rows // group <= 2 * UNROLL:
        for lag in range(*lags):
            step(lag)
    else:
        lax.fori_loop(*lags, lambda lag, none: (step(lag), none)[1], 0)


def fold_lines(lines, dtaps, row):
    here = lax.broadcasted_iota(jnp.int32, (dtaps.shape[0], WIDTH), 0) == row
    for j in range(lines.shape[0]):
        lanes = slice(j * WIDTH, (j + 1) * WIDTH)
        total = jnp.broadcast_to(jnp.sum(lines[j], axis=0, keepdims=True), here.shape)
        dtaps[:, lanes] = jnp.where(here, total, dtaps[:, lanes])


def row_at(many, n):
    return pl.program_id(1) * many + n


def row_of(taps, many, n):
    row = row_at(many, n)
    return lambda lanes: taps[pl.ds(row, 1), lanes]


def lead_kernel(blocks, group, many, role, x, taps, bias, out, xs, acc, *tiles):
    pairs = blocks // 2
    rows = pairs * group

    def each(case, n):
        place = pl.ds(pl.multiple_of(n * group, group), group)
        line, band = xs, tiles
        line[0:rows, :] = jnp.zeros((rows, WIDE), BF16)
        gather_rows(case, x.at[:, place], line, rows, blocks, group)
        build_band(row_of(taps, many, n), band, case, blocks)
        value = apply_band(line, rows, -1, 0, (0, pairs), band, case, False, acc, group)
        value += bias_term(line[rows : 2 * rows, :], bias[place], pairs, group)
        scatter_rows(case, value, out.at[:, place], blocks, group)

    pick(role[0], lambda case: sweep(many, functools.partial(each, case)))


def local_kernel(
    blocks, group, many, role, x, y, taps, bias, out, dtaps, dbias, xs, ys, yl, acc, lines, *tiles
):
    pairs = blocks // 2
    rows = pairs * group

    def each(case, n):
        place = pl.ds(pl.multiple_of(n * group, group), group)
        ys[rows : 2 * rows, :] = jnp.zeros((rows, WIDE), BF16)
        yl[2 * rows : 4 * rows, :] = jnp.zeros((2 * rows, WIDTH), BF16)
        gather_line(case, x.at[:, place], xs, 0, blocks, group)
        gather_rows(case, y.at[:, place], ys, 0, blocks, group)
        gather_line(case, y.at[:, place], yl, 0, blocks, group)
        build_band(row_of(taps, many, n), tiles, 1 - case, blocks)
        value = apply_band(ys, 0, 1, 0, (0, pairs), tiles, 1 - case, True, acc, group)
        out[n] = value + bias_term(ys[0:rows, :], bias[place], pairs, group)
        both = xs[...].astype(F32) * yl[0 : 2 * rows, :].astype(F32)
        dbias[place] = jnp.sum(both.reshape(blocks, group, WIDTH), axis=0)
        lines[...] = jnp.zeros_like(lines)
        correlate(case, flip_rows(xs[...]), yl, 0, 0, (0, blocks), 2 * blocks, lines, group)
        fold_lines(lines, dtaps, row_at(many, n))

    pick(role[0], lambda case: sweep(many, functools.partial(each, case)))


def cross_kernel(blocks, group, many, role, r_a, r_b, taps, base, out, rs, acc, *tiles):
    pairs = blocks // 2
    rows = pairs * group

    def each(case, n):
        place = pl.ds(pl.multiple_of(n * group, group), group)
        zeros = jnp.zeros((rows, WIDE), BF16)
        rs[0:rows, :] = zeros
        rs[2 * rows : 3 * rows, :] = zeros
        begins = pl.program_id(0) == 0
        for i in range(blocks):
            at = i if case == 0 else blocks - 1 - i
            row = rows + (i // 2) * group
            col = (i % 2) * WIDTH
            tile = jnp.where(begins, r_a[at, place, :], r_b[at, place, :])
            rs[row : row + group, col : col + WIDTH] = tile
        build_band(row_of(taps, many, n), tiles, 1 - case, 2 * blocks)
        value = apply_band(
            rs, rows, 1, -pairs, (1, 2 * pairs), tiles, 1 - case, True, acc, group, base.at[n]
        )
        scatter_rows(case, value, out.at[:, place], blocks, group)

    pick(role[0], lambda case: sweep(many, functools.partial(each, case)))


def remote_kernel(blocks, group, many, role, x, r_a, r_b, dtaps, xs, rl, lines):
    rows = blocks * group

    def each(case, n):
        place = pl.ds(pl.multiple_of(n * group, group), group)
        zeros = jnp.zeros((rows, WIDTH), BF16)
        rl[0:rows, :] = zeros
        rl[2 * rows : 3 * rows, :] = zeros
        gather_line(case, x.at[:, case, place], xs, 0, blocks, group)
        r = r_a if case == 0 else r_b
        gather_line(case, r.at[:, place], rl, rows, blocks, group)
        lines[...] = jnp.zeros_like(lines)
        correlate(
            case, flip_rows(xs[...]), rl, rows, -blocks, (1, 2 * blocks), 2 * blocks, lines, group
        )
        fold_lines(lines, dtaps, row_at(many, n))

    pick(role[0], lambda case: sweep(many, functools.partial(each, case)))


class Sizes:
    def __init__(self, x, taps, group):
        self.group = group
        self.blocks, _, self.per, self.tokens = x.shape
        self.groups, self.width = taps.shape[1:]
        self.many = min(self.groups, MANY)
        self.rows = self.blocks // 2 * group
        self.data = pl.BlockSpec(
            (self.blocks, None, self.many * group, self.tokens), lambda p, i, s: (0, p, i, 0)
        )
        self.both = pl.BlockSpec(
            (self.blocks, 2, self.many * group, self.tokens), lambda p, i, s: (0, 0, i, 0)
        )
        self.bands = [pltpu.VMEM((WIDTH, self.width), BF16)] * TAP_PARTS
        self.acc = pltpu.VMEM((self.rows, WIDE), F32)
        self.lines = pltpu.VMEM((self.width // WIDTH, 8, WIDTH), F32)
        self.stream = jax.ShapeDtypeStruct(x.shape, BF16)
        self.sums = jax.ShapeDtypeStruct((2, self.groups, self.rows, WIDE), F32)
        self.sums_spec = pl.BlockSpec(
            (None, self.many, self.rows, WIDE), lambda p, i, s: (p, i, 0, 0)
        )
        self.taps = pl.BlockSpec((None, self.groups, self.width), lambda p, i, s: (p, 0, 0))
        self.bias = pl.BlockSpec((None, self.many * group, WIDTH), lambda p, i, s: (p, i, 0))

    def held(self, count, width=WIDE):
        return pltpu.VMEM((count * self.rows, width), BF16)

    def dtaps(self, parts):
        return jax.ShapeDtypeStruct((parts, self.groups, self.width), F32)

    def call(self, kernel, parts, out_shape, in_specs, out_specs, scratch, share):
        work = 4 * self.groups * self.group * (self.blocks * self.tokens) ** 2
        return pl.pallas_call(
            functools.partial(kernel, self.blocks, self.group, self.many),
            out_shape=out_shape,
            grid_spec=pltpu.PrefetchScalarGridSpec(
                num_scalar_prefetch=1,
                grid=(parts, self.groups // self.many),
                in_specs=in_specs,
                out_specs=out_specs,
                scratch_shapes=scratch,
            ),
            cost_estimate=pl.CostEstimate(
                flops=int(share * work),
                bytes_accessed=8 * self.blocks * self.per * self.tokens,
                transcendentals=0,
            ),
        )


def lead(role, x, taps, bias, group):
    z = Sizes(x, taps, group)
    return z.call(
        lead_kernel, 2, z.stream, [z.data, z.taps, z.bias], z.data,
        [z.held(2), z.acc] + z.bands, 1,
    )(role, x, taps, bias)


def local_part(role, x, y, taps, bias, group):
    z = Sizes(x, taps, group)
    return z.call(
        local_kernel, 2,
        (z.sums, z.dtaps(2), jax.ShapeDtypeStruct((2, z.per, WIDTH), F32)),
        [z.data, z.data, z.taps, z.bias],
        (z.sums_spec, z.taps, z.bias),
        [z.held(2, WIDTH), z.held(2), z.held(4, WIDTH), z.acc, z.lines] + z.bands, 1.5,
    )(role, x, y, taps, bias)


def cross_part(role, x, r_a, r_b, taps, base, group):
    z = Sizes(x, taps, group)
    last = z.groups // z.many - 1
    shape = (z.blocks, z.many * group, z.tokens)
    spec_a = pl.BlockSpec(shape, lambda p, i, s: (0, jnp.where(p == 0, i, last), 0))
    spec_b = pl.BlockSpec(shape, lambda p, i, s: (0, jnp.where(p == 1, i, 0), 0))
    return z.call(
        cross_kernel, 2, z.stream, [spec_a, spec_b, z.taps, z.sums_spec], z.data,
        [z.held(3), z.acc] + z.bands, 2,
    )(role, r_a, r_b, taps, base)


def remote_part(role, x, r_a, r_b, taps, group):
    z = Sizes(x, taps, group)
    spec = pl.BlockSpec((z.blocks, z.many * group, z.tokens), lambda p, i, s: (0, i, 0))
    return z.call(
        remote_kernel, 1, z.dtaps(1), [z.both, spec, spec], z.taps,
        [z.held(2, WIDTH), z.held(6, WIDTH), z.lines], 1,
    )(role, x, r_a, r_b)


def exact_parts(data):
    high = data.astype(BF16)
    rest = data - high.astype(F32)
    middle = rest.astype(BF16)
    return high, middle, (rest - middle.astype(F32)).astype(BF16)


def reverse_line(data, length, count):
    rows, width = data.shape
    total = length // WIDTH
    down = lax.broadcasted_iota(jnp.int32, (WIDTH, WIDTH), 0)
    across = lax.broadcasted_iota(jnp.int32, (WIDTH, WIDTH), 1)
    inner = jnp.where(down + across == WIDTH, 1.0, 0.0).astype(BF16)
    edge = jnp.where(down + across == 0, 1.0, 0.0).astype(BF16)
    zero = jnp.zeros((rows, WIDTH), F32)

    def block(t):
        return data[:, t * WIDTH : (t + 1) * WIDTH] if 0 <= t < width // WIDTH else zero

    done = []
    for j in range(count // WIDTH):
        found = zero
        for a, b in zip(exact_parts(block(total - 1 - j)), exact_parts(block(total - j))):
            found += dot(a, inner) + dot(b, edge)
        done.append(found)
    return jnp.concatenate(done, axis=1)


def arrange_kernel(role, mine, other, my_bias, other_bias, lead_taps, follow_taps, bias):
    groups, length = mine.shape

    def main(case):
        for part in (0, 1):
            taps = (mine if part == case else other)[...]
            ahead = jnp.concatenate([jnp.zeros((groups, WIDTH), F32), taps], axis=1)
            behind = reverse_line(taps, length, length + WIDTH)
            first, second = (ahead, behind) if case == 0 else (behind, ahead)
            lead_taps[part] = first
            follow_taps[part] = second
            line = (my_bias if part == case else other_bias)[...]
            bias[part] = jnp.broadcast_to(line, (WIDTH, line.shape[1])).T

    pick(role[0], main)


def natural(case, dtaps, count):
    if case == 0:
        return dtaps[:, WIDTH : WIDTH + count]
    return reverse_line(dtaps, dtaps.shape[1] - WIDTH, count)


def channel_line(dbias):
    square = dbias[...]
    if square.shape[0] < WIDTH:
        square = jnp.concatenate(
            [square, jnp.zeros((WIDTH - square.shape[0], WIDTH), F32)], axis=0
        )
    return jnp.sum(square.T, axis=0, keepdims=True)


def send_kernel(role, dtaps, dbias, sent):
    _, groups, width = dtaps.shape
    half = (width - WIDTH) // 2

    def main(case):
        sent[:, :half] = natural(case, dtaps[1 - case], half)
        sent[:, half:] = jnp.broadcast_to(channel_line(dbias.at[1 - case]), (groups, WIDTH))

    pick(role[0], main)


def receive_kernel(role, dtaps, dbias, far, came, grad_taps, grad_bias):
    length = dtaps.shape[2] - WIDTH
    half = length // 2

    def main(case):
        total = natural(case, dtaps[case] + far[0], length)
        grad_taps[:, :half] = total[:, :half] + came[:, :half]
        grad_taps[:, half:] = total[:, half:]
        grad_bias[...] = channel_line(dbias.at[case]) + came[0:1, half:]

    pick(role[0], main)


def whole_call(kernel, out_shape, *args):
    spec = lambda a: pl.BlockSpec(a.shape, lambda i, s: (0,) * len(a.shape))
    outs = out_shape if isinstance(out_shape, tuple) else (out_shape,)
    return pl.pallas_call(
        kernel,
        out_shape=out_shape,
        grid_spec=pltpu.PrefetchScalarGridSpec(
            num_scalar_prefetch=1,
            grid=(1,),
            in_specs=[spec(a) for a in args[1:]],
            out_specs=tuple(spec(o) for o in outs) if isinstance(out_shape, tuple) else spec(out_shape),
        ),
    )(*args)


def exchange(values):
    return lax.all_to_all(values, RING, split_axis=0, concat_axis=0)


def local(queries, key_stream, value_stream, filters, bias, grad_out):
    ranks = lax.axis_size(RING)
    role = lax.axis_index("half").astype(jnp.int32)[None]
    groups, length = filters.shape
    per = bias.shape[0]
    group = per // groups
    partner = [(i, (i + ranks) % (2 * ranks)) for i in range(2 * ranks)]
    swap = lambda a: lax.ppermute(a, ("half",) + RING, partner)

    bias = bias[None]
    other = swap(filters)
    other_bias = swap(bias)
    x, y = prepare(role, queries, key_stream, value_stream, grad_out, ranks)
    x = exchange(x)
    y = exchange(y)
    taps = jax.ShapeDtypeStruct((2, groups, length + WIDTH), F32)
    lead_taps, follow_taps, offsets = whole_call(
        arrange_kernel,
        (taps, taps, jax.ShapeDtypeStruct((2, per, WIDTH), F32)),
        role, filters, other, bias, other_bias,
    )
    r_a = swap(x[:, 0])
    r_b = swap(x[:, 1])
    one = lead(role, x, lead_taps, offsets, group)
    one = exchange(one)
    two, dtaps, dbias = local_part(role, x, y, follow_taps, offsets, group)
    half = jax.ShapeDtypeStruct((groups, length // 2 + WIDTH), F32)
    sent = whole_call(send_kernel, half, role, dtaps, dbias)
    came = swap(sent)
    two = cross_part(role, x, r_a, r_b, follow_taps, two, group)
    two = exchange(two)
    far = remote_part(role, x, r_a, r_b, follow_taps, group)
    grad_filters, grad_bias = whole_call(
        receive_kernel,
        (jax.ShapeDtypeStruct((groups, length), F32), jax.ShapeDtypeStruct((1, WIDTH), F32)),
        role, dtaps, dbias, far, came,
    )
    outs = finish(role, queries, key_stream, value_stream, grad_out, one, two, ranks)
    return (*outs, grad_filters, grad_bias[0, :per])


def solution(mesh):
    ctx, dp = mesh.devices.shape
    split = Mesh(mesh.devices.reshape(2, ctx // 2, dp), ("half", "ctx_low", "dp"))
    axes = ("half", "ctx_low", "dp")
    stream = P(None, axes)
    return jax.shard_map(
        local,
        mesh=split,
        in_specs=(stream, stream, stream, P(axes, None), P(axes), stream),
        out_specs=(stream, stream, stream, stream, P(axes, None), P(axes)),
        check_vma=False,
    )
```

profile of v0, /device:TPU:0, one launch (start us, length us, event | category | flops | bytes accessed | tf_op | source)
XLA Modules:
  0.0 158.8 jit_solution(16912096705965877105)
XLA Ops:
  0.6 3.4 %prepare.1 = (bf16[16,2,128,128]{3,2,1,0:T(8,128)(2,1)}, bf16[16,2,128,128]{3,2,1,0:T(8,128)(2,1)}) custom-call(s32[1]{0:T(128)} %bitcast.role, bf16[2,16,128,128]{3,2,1,0:T(8,128)(2,1)} %bitcast.19, bf16[2,16,128,128]{3,2,1,0:T(8,128)(2,1)} %bitcast.21, bf16[2,16,128,128]{3,2,1,0:T(8,128)(2,1)} %bitcast.23, bf16[2,16,128,128]{3,2,1,0:T(8,128)(2,1)} %bitcast.25), custom_call_target="tpu_custom_call" | custom-call | tf_op jit(solution)/shard_map/prepare/pallas_call | solution.py:49
  4.0 21.9 %all_to_all.20.x = bf16[16,2,128,128]{3,2,1,0:T(8,128)(2,1)} all-to-all(bf16[16,2,128,128]{3,2,1,0:T(8,128)(2,1)} %get-tuple-element.20), channel_id=1, replica_groups=mesh['half'=2,'ctx_low'=8,'dp'=2] {'ctx_low','dp'}, dimensions={0} | all-to-all | bytes 2097152 | tf_op jit(solution)/shard_map/all_to_all | solution.py:533
  25.9 3.7 %all-to-all-start.2 = ((bf16[16,2,128,128]{3,2,1,0:T(8,128)(2,1)}), bf16[16,2,128,128]{3,2,1,0:T(8,128)(2,1)S(1)}, u32[]{:S(2)}, u32[]{:S(2)}) async-start(bf16[16,2,128,128]{3,2,1,0:T(8,128)(2,1)} %get-tuple-element.24), calls=%async_computation.2 | async-start | bytes 2097152 | tf_op jit(solution)/shard_map/all_to_all | solution.py:533
  29.6 2.7 %collective-permute-start = (f32[8,4096]{1,0:T(8,128)S(1)}, f32[8,4096]{1,0:T(8,128)S(1)}, u32[]{:S(2)}, u32[]{:S(2)}) collective-permute-start(f32[8,4096]{1,0:T(8,128)S(1)} %copy-done.4), channel_id=1, source_target_pairs={{0,16},{1,17},{2,18},{3,19},{4,20},{5,21},{6,22},{7,23},{8,24},{9,... | collective-permute-start | bytes 393224 | tf_op jit(solution)/shard_map/ppermute | solution.py:543
  32.6 13.1 %collective-permute-done.1.other_bias = f32[1,128]{1,0:T(1,128)S(1)} collective-permute-done((f32[1,128]{1,0:T(1,128)S(1)}, f32[1,128]{1,0:T(1,128)S(1)}, u32[]{:S(2)}, u32[]{:S(2)}) %collective-permute-start.1) | collective-permute-done | bytes 544 | tf_op jit(solution)/shard_map/ppermute | solution.py:543
  46.2 0.7 copy-done.5
  46.9 4.2 %shard_map.109 = (f32[2,8,4224]{2,1,0:T(8,128)}, f32[2,8,4224]{2,1,0:T(8,128)}, f32[2,128,128]{2,1,0:T(8,128)}) custom-call(s32[1]{0:T(128)} %bitcast.role, f32[8,4096]{1,0:T(8,128)} %mine.1, f32[8,4096]{1,0:T(8,128)} %copy-done.5, f32[1,128]{1,0:T(1,128)} %bitcast.27, f32[1,128]{1,0:T(1,128)} %copy-done.8), custom_call_target="tpu_custom_call" | custom-call | tf_op jit(solution)/shard_map/pallas_call | solution.py:520
  51.1 8.0 %shard_map.110 = bf16[16,2,128,128]{3,2,1,0:T(8,128)(2,1)} custom-call(s32[1]{0:T(128)} %bitcast.role, bf16[16,2,128,128]{3,2,1,0:T(8,128)(2,1)} %all_to_all.20.x, f32[2,8,4224]{2,1,0:T(8,128)} %get-tuple-element.21.taps, f32[2,128,128]{2,1,0:T(8,128)} %get-tuple-element.22.bias), custom_call_target="tpu_custom_call" | custom-call | flops 2147483648 | bytes 2097152 | tf_op jit(solution)/shard_map/pallas_call | solution.py:395
  59.1 7.1 %all-to-all-start.1 = ((bf16[16,2,128,128]{3,2,1,0:T(8,128)(2,1)}), bf16[16,2,128,128]{3,2,1,0:T(8,128)(2,1)S(1)}, u32[]{:S(2)}, u32[]{:S(2)}) async-start(bf16[16,2,128,128]{3,2,1,0:T(8,128)(2,1)} %shard_map.110), calls=%async_computation.1 | async-start | bytes 2097152 | tf_op jit(solution)/shard_map/all_to_all | solution.py:533
  66.2 1.0 slice_bitcast_fusion
  67.5 2.7 %collective-permute-start.3 = (bf16[16,128,128]{2,1,0:T(8,128)(2,1)}, bf16[16,128,128]{2,1,0:T(8,128)(2,1)S(1)}, u32[]{:S(2)}, u32[]{:S(2)}) collective-permute-start(bf16[16,128,128]{2,1,0:T(8,128)(2,1)} %get-tuple-element.34), channel_id=1, source_target_pairs={{0,16},{1,17},{2,18},{3,19},{4,20},{5,21},{6,22},{7,23},{8,24},{9,... | collective-permute-start | bytes 1572872 | tf_op jit(solution)/shard_map/ppermute | solution.py:543
  70.2 14.2 %shard_map.111 = (f32[2,8,128,256]{3,2,1,0:T(8,128)}, f32[2,8,4224]{2,1,0:T(8,128)}, f32[2,128,128]{2,1,0:T(8,128)}) custom-call(s32[1]{0:T(128)} %bitcast.role, bf16[16,2,128,128]{3,2,1,0:T(8,128)(2,1)} %all_to_all.20.x, bf16[16,2,128,128]{3,2,1,0:T(8,128)(2,1)} %copy-done.3, f32[2,8,4224]{2,1,0:T(8,128)} %get-tuple-element.23.taps, ...), custom_call_target="tpu_custom_call" | custom-call | flops 3221225472 | bytes 2097152 | tf_op jit(solution)/shard_map/pallas_call | solution.py:403
  84.4 21.3 %collective-permute-done.2.r_a = bf16[16,128,128]{2,1,0:T(8,128)(2,1)S(1)} collective-permute-done((bf16[16,128,128]{2,1,0:T(8,128)(2,1)}, bf16[16,128,128]{2,1,0:T(8,128)(2,1)S(1)}, u32[]{:S(2)}, u32[]{:S(2)}) %collective-permute-start.2) | collective-permute-done | bytes 524320 | tf_op jit(solution)/shard_map/ppermute | solution.py:543
  105.7 10.7 %collective-permute-done.3.r_b = bf16[16,128,128]{2,1,0:T(8,128)(2,1)S(1)} collective-permute-done((bf16[16,128,128]{2,1,0:T(8,128)(2,1)}, bf16[16,128,128]{2,1,0:T(8,128)(2,1)S(1)}, u32[]{:S(2)}, u32[]{:S(2)}) %collective-permute-start.3) | collective-permute-done | bytes 524320 | tf_op jit(solution)/shard_map/ppermute | solution.py:543
  116.4 0.8 copy-done.10
  117.2 14.6 %shard_map.112 = bf16[16,2,128,128]{3,2,1,0:T(8,128)(2,1)} custom-call(s32[1]{0:T(128)} %bitcast.role, bf16[16,128,128]{2,1,0:T(8,128)(2,1)} %copy-done.9, bf16[16,128,128]{2,1,0:T(8,128)(2,1)} %copy-done.10, f32[2,8,4224]{2,1,0:T(8,128)} %get-tuple-element.23.taps, f32[2,8,128,256]{3,2,1,0:T(8,128)} %get-tuple-element.25.base), custom_call_target="tpu_custom_call" | custom-call | flops 4294967296 | bytes 2097152 | tf_op jit(solution)/shard_map/pallas_call | solution.py:418
  131.7 3.9 %all-to-all-start.3 = ((bf16[16,2,128,128]{3,2,1,0:T(8,128)(2,1)}), bf16[16,2,128,128]{3,2,1,0:T(8,128)(2,1)S(1)}, u32[]{:S(2)}, u32[]{:S(2)}) async-start(bf16[16,2,128,128]{3,2,1,0:T(8,128)(2,1)} %shard_map.112), calls=%async_computation.3 | async-start | bytes 2097152 | tf_op jit(solution)/shard_map/all_to_all | solution.py:533
  135.7 1.9 %shard_map.114 = f32[8,2176]{1,0:T(8,128)} custom-call(s32[1]{0:T(128)} %bitcast.role, f32[2,8,4224]{2,1,0:T(8,128)} %get-tuple-element.30.dtaps, f32[2,128,128]{2,1,0:T(8,128)} %get-tuple-element.31.dbias), custom_call_target="tpu_custom_call" | custom-call | tf_op jit(solution)/shard_map/pallas_call | solution.py:520
  137.6 0.7 collective-permute-start.4
  138.3 7.8 %shard_map.113.far = f32[1,8,4224]{2,1,0:T(8,128)} custom-call(s32[1]{0:T(128)} %bitcast.role, bf16[16,2,128,128]{3,2,1,0:T(8,128)(2,1)} %all_to_all.20.x, bf16[16,128,128]{2,1,0:T(8,128)(2,1)} %copy-done.9, bf16[16,128,128]{2,1,0:T(8,128)(2,1)} %copy-done.10), custom_call_target="tpu_custom_call" | custom-call | flops 2147483648 | bytes 2097152 | tf_op jit(solution)/shard_map/pallas_call | solution.py:427
  146.2 4.6 %collective-permute-done.4.came = f32[8,2176]{1,0:T(8,128)S(1)} collective-permute-done((f32[8,2176]{1,0:T(8,128)}, f32[8,2176]{1,0:T(8,128)S(1)}, u32[]{:S(2)}, u32[]{:S(2)}) %collective-permute-start.4) | collective-permute-done | bytes 69664 | tf_op jit(solution)/shard_map/ppermute | solution.py:543
  151.4 1.9 %shard_map.115 = (f32[8,4096]{1,0:T(8,128)}, f32[1,128]{1,0:T(1,128)}) custom-call(s32[1]{0:T(128)} %bitcast.role, f32[2,8,4224]{2,1,0:T(8,128)} %get-tuple-element.30.dtaps, f32[2,128,128]{2,1,0:T(8,128)} %get-tuple-element.31.dbias, f32[1,8,4224]{2,1,0:T(8,128)} %shard_map.113.far, f32[8,2176]{1,0:T(8,128)} %copy-done.6), custom_call_target="tpu_custom_call" | custom-call | tf_op jit(solution)/shard_map/pallas_call | solution.py:520
  153.3 0.9 copy-done.1
  154.3 4.6 %finish.1 = (bf16[2,16,128,128]{3,2,1,0:T(8,128)(2,1)}, bf16[2,16,128,128]{3,2,1,0:T(8,128)(2,1)}, bf16[2,16,128,128]{3,2,1,0:T(8,128)(2,1)}, bf16[2,16,128,128]{3,2,1,0:T(8,128)(2,1)}) custom-call(s32[1]{0:T(128)} %bitcast.role, bf16[2,16,128,128]{3,2,1,0:T(8,128)(2,1)} %bitcast.20, bf16[2,16,128,128]{3,2,1,0:T(8,128)(2,1)} %bitcast.22, ...), custom_call_target="tpu_custom_call" | custom-call | tf_op jit(solution)/shard_map/finish/pallas_call | solution.py:81
  (25 shorter events, 1.8 us)
Async XLA Ops:
  4.0 25.5 %copy-start.4 = (f32[8,4096]{1,0:T(8,128)S(1)}, f32[8,4096]{1,0:T(8,128)}, u32[]{:S(2)}) copy-start(f32[8,4096]{1,0:T(8,128)} %mine.1) | copy-start | bytes 393220
  4.0 28.2 %copy-start.7 = (f32[128]{0:T(128)S(1)}, f32[128]{0:T(128)}, u32[]{:S(2)}) copy-start(f32[128]{0:T(128)} %param.10) | copy-start | bytes 1540
  25.9 33.2 %all-to-all-start.2 = ((bf16[16,2,128,128]{3,2,1,0:T(8,128)(2,1)}), bf16[16,2,128,128]{3,2,1,0:T(8,128)(2,1)S(1)}, u32[]{:S(2)}, u32[]{:S(2)}) async-start(bf16[16,2,128,128]{3,2,1,0:T(8,128)(2,1)} %get-tuple-element.24), calls=%async_computation.2 | async-start | bytes 2097152 | tf_op jit(solution)/shard_map/all_to_all | solution.py:533
  29.6 16.1 %collective-permute-start = (f32[8,4096]{1,0:T(8,128)S(1)}, f32[8,4096]{1,0:T(8,128)S(1)}, u32[]{:S(2)}, u32[]{:S(2)}) collective-permute-start(f32[8,4096]{1,0:T(8,128)S(1)} %copy-done.4), channel_id=1, source_target_pairs={{0,16},{1,17},{2,18},{3,19},{4,20},{5,21},{6,22},{7,23},{8,24},{9,... | collective-permute-start | bytes 393224 | tf_op jit(solution)/shard_map/ppermute | solution.py:543
  32.2 13.5 %collective-permute-start.1 = (f32[1,128]{1,0:T(1,128)S(1)}, f32[1,128]{1,0:T(1,128)S(1)}, u32[]{:S(2)}, u32[]{:S(2)}) collective-permute-start(f32[1,128]{1,0:T(1,128)S(1)} %bitcast.28), channel_id=1, source_target_pairs={{0,16},{1,17},{2,18},{3,19},{4,20},{5,21},{6,22},{7,23},{8,24},{9,... | collective-permute-start | bytes 1544 | tf_op jit(solution)/shard_map/ppermute | solution.py:543
  45.7 0.5 copy-start.8
  46.2 0.7 copy-start.5
  59.1 7.1 %copy-start.2 = (bf16[16,2,128,128]{3,2,1,0:T(8,128)(2,1)S(1)}, bf16[16,2,128,128]{3,2,1,0:T(8,128)(2,1)}, u32[]{:S(2)}) copy-start(bf16[16,2,128,128]{3,2,1,0:T(8,128)(2,1)} %all_to_all.20.x) | copy-start | bytes 3145732
  59.1 8.2 %copy-start.3 = (bf16[16,2,128,128]{3,2,1,0:T(8,128)(2,1)}, bf16[16,2,128,128]{3,2,1,0:T(8,128)(2,1)S(1)}, u32[]{:S(2)}) copy-start(bf16[16,2,128,128]{3,2,1,0:T(8,128)(2,1)S(1)} %all-to-all-done.2.y) | copy-start | bytes 3145732
  59.1 72.6 %all-to-all-start.1 = ((bf16[16,2,128,128]{3,2,1,0:T(8,128)(2,1)}), bf16[16,2,128,128]{3,2,1,0:T(8,128)(2,1)S(1)}, u32[]{:S(2)}, u32[]{:S(2)}) async-start(bf16[16,2,128,128]{3,2,1,0:T(8,128)(2,1)} %shard_map.110), calls=%async_computation.1 | async-start | bytes 2097152 | tf_op jit(solution)/shard_map/all_to_all | solution.py:533
  67.3 38.4 %collective-permute-start.2 = (bf16[16,128,128]{2,1,0:T(8,128)(2,1)}, bf16[16,128,128]{2,1,0:T(8,128)(2,1)S(1)}, u32[]{:S(2)}, u32[]{:S(2)}) collective-permute-start(bf16[16,128,128]{2,1,0:T(8,128)(2,1)} %get-tuple-element.35), channel_id=1, source_target_pairs={{0,16},{1,17},{2,18},{3,19},{4,20},{5,21},{6,22},{7,23},{8,24},{9,... | collective-permute-start | bytes 1572872 | tf_op jit(solution)/shard_map/ppermute | solution.py:543
  67.5 48.8 %collective-permute-start.3 = (bf16[16,128,128]{2,1,0:T(8,128)(2,1)}, bf16[16,128,128]{2,1,0:T(8,128)(2,1)S(1)}, u32[]{:S(2)}, u32[]{:S(2)}) collective-permute-start(bf16[16,128,128]{2,1,0:T(8,128)(2,1)} %get-tuple-element.34), channel_id=1, source_target_pairs={{0,16},{1,17},{2,18},{3,19},{4,20},{5,21},{6,22},{7,23},{8,24},{9,... | collective-permute-start | bytes 1572872 | tf_op jit(solution)/shard_map/ppermute | solution.py:543
  105.7 10.7 %copy-start.9 = (bf16[16,128,128]{2,1,0:T(8,128)(2,1)}, bf16[16,128,128]{2,1,0:T(8,128)(2,1)S(1)}, u32[]{:S(2)}) copy-start(bf16[16,128,128]{2,1,0:T(8,128)(2,1)S(1)} %collective-permute-done.2.r_a) | copy-start | bytes 1572868
  116.4 0.8 copy-start.10
  131.7 14.4 %copy-start = (bf16[16,2,128,128]{3,2,1,0:T(8,128)(2,1)}, bf16[16,2,128,128]{3,2,1,0:T(8,128)(2,1)S(1)}, u32[]{:S(2)}) copy-start(bf16[16,2,128,128]{3,2,1,0:T(8,128)(2,1)S(1)} %all-to-all-done.1.one) | copy-start | bytes 3145732
  131.7 21.6 %all-to-all-start.3 = ((bf16[16,2,128,128]{3,2,1,0:T(8,128)(2,1)}), bf16[16,2,128,128]{3,2,1,0:T(8,128)(2,1)S(1)}, u32[]{:S(2)}, u32[]{:S(2)}) async-start(bf16[16,2,128,128]{3,2,1,0:T(8,128)(2,1)} %shard_map.112), calls=%async_computation.3 | async-start | bytes 2097152 | tf_op jit(solution)/shard_map/all_to_all | solution.py:533
  137.6 13.2 %collective-permute-start.4 = (f32[8,2176]{1,0:T(8,128)}, f32[8,2176]{1,0:T(8,128)S(1)}, u32[]{:S(2)}, u32[]{:S(2)}) collective-permute-start(f32[8,2176]{1,0:T(8,128)} %shard_map.114), channel_id=1, source_target_pairs={{0,16},{1,17},{2,18},{3,19},{4,20},{5,21},{6,22},{7,23},{8,24},{9,... | collective-permute-start | bytes 208904 | tf_op jit(solution)/shard_map/ppermute | solution.py:543
  150.8 0.6 copy-start.6
  153.3 0.9 copy-start.1
where the time goes:
time: 160 us; the launch traced here: 159 us
  Pallas kernels  60.6 us (38%)
  waiting for transfers between devices  49.7 us (31%)
  blocking collectives  21.9 us (14%)
  starting transfers between devices  21.3 us (13%)
  local copies, waits for them, and re-layouts  4.59 us (3%)
    ppermute x5, waiting for transfers between devices, local(): swap = lambda a: lax.ppermute(a, ('half',) + RING, partner)  49.7 us
    all_to_all x1, blocking collectives, exchange(): return lax.all_to_all(values, RING, split_axis=0, concat_axis=0)  21.9 us
    all_to_all x3, starting transfers between devices, exchange(): return lax.all_to_all(values, RING, split_axis=0, concat_axis=0)  14.7 us
    pallas_call x1, Pallas kernels, cross_part(): z.call(cross_kernel, 2, z.stream, [spec_a, spec_b, z.taps, z.sums_spec],...  14.6 us
    pallas_call x1, Pallas kernels, local_part(): z.call(local_kernel, 2, (z.sums, z.dtaps(2), jax.ShapeDtypeStruct((2, z.p...  14.2 us
    pallas_call x3, Pallas kernels, whole_call(): pl.pallas_call(kernel, out_shape=out_shape, grid_spec=pltpu.PrefetchScala...  8.05 us
    pallas_call x1, Pallas kernels, lead(): z.call(lead_kernel, 2, z.stream, [z.data, z.taps, z.bias], z.data, [z.hel...  8.01 us
    pallas_call x1, Pallas kernels, remote_part(): z.call(remote_kernel, 1, z.dtaps(1), [z.both, spec, spec], z.taps, [z.hel...  7.82 us
  transfers between devices with their start and end apart: 8, of which 4 were waited for; matrix products, arithmetic and copies ran while one was open for 1% of the time, Pallas kernels for 33%

commit v1 on v0

--- a/solution.py
+++ b/solution.py
@@ -27,33 +27,32 @@
         pl.when(role == case)(functools.partial(cases, case))
 
 
-def prepare_kernel(role, q, k, v, g, first, own):
+def prepare_kernel(other, role, q, k, v, g, out):
     def main(case):
-        product = (k[...].astype(F32) * v[...].astype(F32)).astype(BF16)
-        weighted = (q[...].astype(F32) * g[...].astype(F32)).astype(BF16)
-        x, y = (product, weighted) if case == 0 else (weighted, product)
+        one, two = (k, v) if case == other else (q, g)
+        made = (one[...].astype(F32) * two[...].astype(F32)).astype(BF16)
         for part in (0, 1):
-            first[:, part] = x[part]
-            own[:, part] = y[part]
+            out[:, part] = made[part]
 
     pick(role[0], main)
 
 
-def prepare(role, q, k, v, g, ranks):
+def prepare(other, role, q, k, v, g, ranks):
     channels, tokens = q.shape
     per = channels // (2 * ranks)
     view = lambda a: a.reshape(2, ranks, per, tokens)
     step = ranks // STEPS
-    spec = pl.BlockSpec((2, step, per, tokens), lambda h, r: (0, h, 0, 0))
-    out_spec = pl.BlockSpec((step, 2, per, tokens), lambda h, r: (h, 0, 0, 0))
+    block = (2, step, per, tokens)
+    used = pl.BlockSpec(block, lambda h, r: (0, jnp.where(r[0] == other, h, 0), 0, 0))
+    rest = pl.BlockSpec(block, lambda h, r: (0, jnp.where(r[0] == other, 0, h), 0, 0))
     return pl.pallas_call(
-        prepare_kernel,
-        out_shape=(jax.ShapeDtypeStruct((ranks, 2, per, tokens), BF16),) * 2,
+        functools.partial(prepare_kernel, other),
+        out_shape=jax.ShapeDtypeStruct((ranks, 2, per, tokens), BF16),
         grid_spec=pltpu.PrefetchScalarGridSpec(
             num_scalar_prefetch=1,
             grid=(STEPS,),
-            in_specs=[spec] * 4,
-            out_specs=(out_spec,) * 2,
+            in_specs=[rest, used, used, rest],
+            out_specs=pl.BlockSpec((step, 2, per, tokens), lambda h, r: (h, 0, 0, 0)),
         ),
         name="prepare",
     )(role, view(q), view(k), view(v), view(g))
@@ -545,7 +544,8 @@
     bias = bias[None]
     other = swap(filters)
     other_bias = swap(bias)
-    x, y = prepare(role, queries, key_stream, value_stream, grad_out, ranks)
+    x = prepare(0, role, queries, key_stream, value_stream, grad_out, ranks)
+    y = prepare(1, role, queries, key_stream, value_stream, grad_out, ranks)
     x = exchange(x)
     y = exchange(y)
     taps = jax.ShapeDtypeStruct((2, groups, length + WIDTH), F32)

time: 160 us -> 160 us (level)
  blocking collectives: 21.9 us -> 0 us
  waiting for transfers between devices: 49.7 us -> 63.3 us
  starting transfers between devices: 21.3 us -> 27.4 us
  Pallas kernels: 60.6 us -> 62.9 us
    all_to_all x1 -> x0, blocking collectives: 21.9 us -> none  [exchange(): return lax.all_to_all(values, RING, split_axis=0, concat_axis=0)]
    all_to_all x3 -> x4, waiting for transfers between devices: 0.01 us -> 13.4 us  [exchange(): return lax.all_to_all(values, RING, split_axis=0, concat_axis=0)]
    all_to_all x3 -> x4, starting transfers between devices: 14.7 us -> 20.4 us  [exchange(): return lax.all_to_all(values, RING, split_axis=0, concat_axis=0)]
    pallas_call x1 -> x2, Pallas kernels: 3.4 us -> 5.63 us  [prepare(): pl.pallas_call(functools.partial(prepare_kernel, other), out_shape=jax.Sh...]
    unnamed x22 -> x24, local copies, waits for them, and re-layouts: 3.55 us -> 3.56 us
  transfers between devices with their start and end apart: 8 -> 9, of which waited for: 4 -> 5; matrix products, arithmetic and copies ran while one was open for 1% -> 1% of each run, Pallas kernels for 33% -> 35%
where the time goes in v1:
time: 160 us; the launch traced here: 159 us
  waiting for transfers between devices  63.3 us (40%)
  Pallas kernels  62.9 us (39%)
  starting transfers between devices  27.4 us (17%)
  local copies, waits for them, and re-layouts  4.61 us (3%)
    ppermute x5, waiting for transfers between devices, local(): swap = lambda a: lax.ppermute(a, ('half',) + RING, partner)  50 us
    all_to_all x4, starting transfers between devices, exchange(): return lax.all_to_all(values, RING, split_axis=0, concat_axis=0)  20.4 us
    pallas_call x1, Pallas kernels, cross_part(): z.call(cross_kernel, 2, z.stream, [spec_a, spec_b, z.taps, z.sums_spec],...  14.6 us
    pallas_call x1, Pallas kernels, local_part(): z.call(local_kernel, 2, (z.sums, z.dtaps(2), jax.ShapeDtypeStruct((2, z.p...  14.2 us
    all_to_all x4, waiting for transfers between devices, exchange(): return lax.all_to_all(values, RING, split_axis=0, concat_axis=0)  13.4 us
    pallas_call x3, Pallas kernels, whole_call(): pl.pallas_call(kernel, out_shape=out_shape, grid_spec=pltpu.PrefetchScala...  8.06 us
    pallas_call x1, Pallas kernels, lead(): z.call(lead_kernel, 2, z.stream, [z.data, z.taps, z.bias], z.data, [z.hel...  8.03 us
    pallas_call x1, Pallas kernels, remote_part(): z.call(remote_kernel, 1, z.dtaps(1), [z.both, spec, spec], z.taps, [z.hel...  7.82 us
  transfers between devices with their start and end apart: 9, of which 5 were waited for; matrix products, arithmetic and copies ran while one was open for 1% of the time, Pallas kernels for 35%

profile of v1, /device:TPU:0, one launch (start us, length us, event | category | flops | bytes accessed | tf_op | source)
XLA Modules:
  0.0 158.9 jit_solution(16585049720385109788)
XLA Ops:
  0.6 2.8 %prepare.2 = bf16[16,2,128,128]{3,2,1,0:T(8,128)(2,1)} custom-call(s32[1]{0:T(128)} %bitcast.role, bf16[2,16,128,128]{3,2,1,0:T(8,128)(2,1)} %bitcast.19, bf16[2,16,128,128]{3,2,1,0:T(8,128)(2,1)} %bitcast.22, bf16[2,16,128,128]{3,2,1,0:T(8,128)(2,1)} %bitcast.25, bf16[2,16,128,128]{3,2,1,0:T(8,128)(2,1)} %bitcast.28), custom_call_target="tpu_custom_call" | custom-call | tf_op jit(solution)/shard_map/prepare/pallas_call | solution.py:48
  3.5 6.3 %all-to-all-start = ((bf16[16,2,128,128]{3,2,1,0:T(8,128)(2,1)}), bf16[16,2,128,128]{3,2,1,0:T(8,128)(2,1)S(1)}, u32[]{:S(2)}, u32[]{:S(2)}) async-start(bf16[16,2,128,128]{3,2,1,0:T(8,128)(2,1)} %prepare.2), calls=%async_computation | async-start | bytes 2097152 | tf_op jit(solution)/shard_map/all_to_all | solution.py:532
  9.8 2.8 %prepare.3 = bf16[16,2,128,128]{3,2,1,0:T(8,128)(2,1)} custom-call(s32[1]{0:T(128)} %bitcast.role, bf16[2,16,128,128]{3,2,1,0:T(8,128)(2,1)} %bitcast.20, bf16[2,16,128,128]{3,2,1,0:T(8,128)(2,1)} %bitcast.23, bf16[2,16,128,128]{3,2,1,0:T(8,128)(2,1)} %bitcast.26, bf16[2,16,128,128]{3,2,1,0:T(8,128)(2,1)} %bitcast.29), custom_call_target="tpu_custom_call" | custom-call | tf_op jit(solution)/shard_map/prepare/pallas_call | solution.py:48
  12.6 13.3 %all-to-all-done.x = bf16[16,2,128,128]{3,2,1,0:T(8,128)(2,1)S(1)} async-done(((bf16[16,2,128,128]{3,2,1,0:T(8,128)(2,1)}), bf16[16,2,128,128]{3,2,1,0:T(8,128)(2,1)S(1)}, u32[]{:S(2)}, u32[]{:S(2)}) %all-to-all-start) | async-done | bytes 1048608 | tf_op jit(solution)/shard_map/all_to_all | solution.py:532
  25.9 3.7 %all-to-all-start.2 = ((bf16[16,2,128,128]{3,2,1,0:T(8,128)(2,1)}), bf16[16,2,128,128]{3,2,1,0:T(8,128)(2,1)S(1)}, u32[]{:S(2)}, u32[]{:S(2)}) async-start(bf16[16,2,128,128]{3,2,1,0:T(8,128)(2,1)} %prepare.3), calls=%async_computation.2 | async-start | bytes 2097152 | tf_op jit(solution)/shard_map/all_to_all | solution.py:532
  29.6 2.7 %collective-permute-start = (f32[8,4096]{1,0:T(8,128)S(1)}, f32[8,4096]{1,0:T(8,128)S(1)}, u32[]{:S(2)}, u32[]{:S(2)}) collective-permute-start(f32[8,4096]{1,0:T(8,128)S(1)} %copy-done.5), channel_id=1, source_target_pairs={{0,16},{1,17},{2,18},{3,19},{4,20},{5,21},{6,22},{7,23},{8,24},{9,... | collective-permute-start | bytes 393224 | tf_op jit(solution)/shard_map/ppermute | solution.py:542
  32.6 13.7 %collective-permute-done.1.other_bias = f32[1,128]{1,0:T(1,128)S(1)} collective-permute-done((f32[1,128]{1,0:T(1,128)S(1)}, f32[1,128]{1,0:T(1,128)S(1)}, u32[]{:S(2)}, u32[]{:S(2)}) %collective-permute-start.1) | collective-permute-done | bytes 544 | tf_op jit(solution)/shard_map/ppermute | solution.py:542
  47.5 4.2 %shard_map.109 = (f32[2,8,4224]{2,1,0:T(8,128)}, f32[2,8,4224]{2,1,0:T(8,128)}, f32[2,128,128]{2,1,0:T(8,128)}) custom-call(s32[1]{0:T(128)} %bitcast.role, f32[8,4096]{1,0:T(8,128)} %mine.1, f32[8,4096]{1,0:T(8,128)} %copy-done.6, f32[1,128]{1,0:T(1,128)} %bitcast.31, f32[1,128]{1,0:T(1,128)} %copy-done.9), custom_call_target="tpu_custom_call" | custom-call | tf_op jit(solution)/shard_map/pallas_call | solution.py:519
  51.7 8.0 %shard_map.110 = bf16[16,2,128,128]{3,2,1,0:T(8,128)(2,1)} custom-call(s32[1]{0:T(128)} %bitcast.role, bf16[16,2,128,128]{3,2,1,0:T(8,128)(2,1)} %copy-done.2, f32[2,8,4224]{2,1,0:T(8,128)} %get-tuple-element.18.taps, f32[2,128,128]{2,1,0:T(8,128)} %get-tuple-element.19.bias), custom_call_target="tpu_custom_call" | custom-call | flops 2147483648 | bytes 2097152 | tf_op jit(solution)/shard_map/pallas_call | solution.py:394
  59.8 6.5 %all-to-all-start.1 = ((bf16[16,2,128,128]{3,2,1,0:T(8,128)(2,1)}), bf16[16,2,128,128]{3,2,1,0:T(8,128)(2,1)S(1)}, u32[]{:S(2)}, u32[]{:S(2)}) async-start(bf16[16,2,128,128]{3,2,1,0:T(8,128)(2,1)} %shard_map.110), calls=%async_computation.1 | async-start | bytes 2097152 | tf_op jit(solution)/shard_map/all_to_all | solution.py:532
  66.3 1.1 slice_bitcast_fusion
  68.2 2.1 %collective-permute-start.3 = (bf16[16,128,128]{2,1,0:T(8,128)(2,1)}, bf16[16,128,128]{2,1,0:T(8,128)(2,1)S(1)}, u32[]{:S(2)}, u32[]{:S(2)}) collective-permute-start(bf16[16,128,128]{2,1,0:T(8,128)(2,1)} %get-tuple-element.30), channel_id=1, source_target_pairs={{0,16},{1,17},{2,18},{3,19},{4,20},{5,21},{6,22},{7,23},{8,24},{9,... | collective-permute-start | bytes 1572872 | tf_op jit(solution)/shard_map/ppermute | solution.py:542
  70.3 14.2 %shard_map.111 = (f32[2,8,128,256]{3,2,1,0:T(8,128)}, f32[2,8,4224]{2,1,0:T(8,128)}, f32[2,128,128]{2,1,0:T(8,128)}) custom-call(s32[1]{0:T(128)} %bitcast.role, bf16[16,2,128,128]{3,2,1,0:T(8,128)(2,1)} %copy-done.2, bf16[16,2,128,128]{3,2,1,0:T(8,128)(2,1)} %copy-done.4, f32[2,8,4224]{2,1,0:T(8,128)} %get-tuple-element.20.taps, ...), custom_call_target="tpu_custom_call" | custom-call | flops 3221225472 | bytes 2097152 | tf_op jit(solution)/shard_map/pallas_call | solution.py:402
  84.5 21.3 %collective-permute-done.2.r_a = bf16[16,128,128]{2,1,0:T(8,128)(2,1)S(1)} collective-permute-done((bf16[16,128,128]{2,1,0:T(8,128)(2,1)}, bf16[16,128,128]{2,1,0:T(8,128)(2,1)S(1)}, u32[]{:S(2)}, u32[]{:S(2)}) %collective-permute-start.2) | collective-permute-done | bytes 524320 | tf_op jit(solution)/shard_map/ppermute | solution.py:542
  105.8 10.7 %collective-permute-done.3.r_b = bf16[16,128,128]{2,1,0:T(8,128)(2,1)S(1)} collective-permute-done((bf16[16,128,128]{2,1,0:T(8,128)(2,1)}, bf16[16,128,128]{2,1,0:T(8,128)(2,1)S(1)}, u32[]{:S(2)}, u32[]{:S(2)}) %collective-permute-start.3) | collective-permute-done | bytes 524320 | tf_op jit(solution)/shard_map/ppermute | solution.py:542
  117.3 14.6 %shard_map.112 = bf16[16,2,128,128]{3,2,1,0:T(8,128)(2,1)} custom-call(s32[1]{0:T(128)} %bitcast.role, bf16[16,128,128]{2,1,0:T(8,128)(2,1)} %copy-done.10, bf16[16,128,128]{2,1,0:T(8,128)(2,1)} %copy-done.11, f32[2,8,4224]{2,1,0:T(8,128)} %get-tuple-element.20.taps, f32[2,8,128,256]{3,2,1,0:T(8,128)} %get-tuple-element.21.base), custom_call_target="tpu_custom_call" | custom-call | flops 4294967296 | bytes 2097152 | tf_op jit(solution)/shard_map/pallas_call | solution.py:417
  131.8 3.9 %all-to-all-start.3 = ((bf16[16,2,128,128]{3,2,1,0:T(8,128)(2,1)}), bf16[16,2,128,128]{3,2,1,0:T(8,128)(2,1)S(1)}, u32[]{:S(2)}, u32[]{:S(2)}) async-start(bf16[16,2,128,128]{3,2,1,0:T(8,128)(2,1)} %shard_map.112), calls=%async_computation.3 | async-start | bytes 2097152 | tf_op jit(solution)/shard_map/all_to_all | solution.py:532
  135.8 1.9 %shard_map.114 = f32[8,2176]{1,0:T(8,128)} custom-call(s32[1]{0:T(128)} %bitcast.role, f32[2,8,4224]{2,1,0:T(8,128)} %get-tuple-element.26.dtaps, f32[2,128,128]{2,1,0:T(8,128)} %get-tuple-element.27.dbias), custom_call_target="tpu_custom_call" | custom-call | tf_op jit(solution)/shard_map/pallas_call | solution.py:519
  137.7 1.1 collective-permute-start.4
  138.8 7.8 %shard_map.113.far = f32[1,8,4224]{2,1,0:T(8,128)} custom-call(s32[1]{0:T(128)} %bitcast.role, bf16[16,2,128,128]{3,2,1,0:T(8,128)(2,1)} %copy-done.2, bf16[16,128,128]{2,1,0:T(8,128)(2,1)} %copy-done.10, bf16[16,128,128]{2,1,0:T(8,128)(2,1)} %copy-done.11), custom_call_target="tpu_custom_call" | custom-call | flops 2147483648 | bytes 2097152 | tf_op jit(solution)/shard_map/pallas_call | solution.py:426
  146.6 4.3 %collective-permute-done.4.came = f32[8,2176]{1,0:T(8,128)S(1)} collective-permute-done((f32[8,2176]{1,0:T(8,128)}, f32[8,2176]{1,0:T(8,128)S(1)}, u32[]{:S(2)}, u32[]{:S(2)}) %collective-permute-start.4) | collective-permute-done | bytes 69664 | tf_op jit(solution)/shard_map/ppermute | solution.py:542
  151.5 1.9 %shard_map.115 = (f32[8,4096]{1,0:T(8,128)}, f32[1,128]{1,0:T(1,128)}) custom-call(s32[1]{0:T(128)} %bitcast.role, f32[2,8,4224]{2,1,0:T(8,128)} %get-tuple-element.26.dtaps, f32[2,128,128]{2,1,0:T(8,128)} %get-tuple-element.27.dbias, f32[1,8,4224]{2,1,0:T(8,128)} %shard_map.113.far, f32[8,2176]{1,0:T(8,128)} %copy-done.7), custom_call_target="tpu_custom_call" | custom-call | tf_op jit(solution)/shard_map/pallas_call | solution.py:519
  153.4 1.0 copy-done.1
  154.4 4.6 %finish.1 = (bf16[2,16,128,128]{3,2,1,0:T(8,128)(2,1)}, bf16[2,16,128,128]{3,2,1,0:T(8,128)(2,1)}, bf16[2,16,128,128]{3,2,1,0:T(8,128)(2,1)}, bf16[2,16,128,128]{3,2,1,0:T(8,128)(2,1)}) custom-call(s32[1]{0:T(128)} %bitcast.role, bf16[2,16,128,128]{3,2,1,0:T(8,128)(2,1)} %bitcast.21, bf16[2,16,128,128]{3,2,1,0:T(8,128)(2,1)} %bitcast.24, ...), custom_call_target="tpu_custom_call" | custom-call | tf_op jit(solution)/shard_map/finish/pallas_call | solution.py:80
  (29 shorter events, 3.8 us)
Async XLA Ops:
  3.5 22.5 %all-to-all-start = ((bf16[16,2,128,128]{3,2,1,0:T(8,128)(2,1)}), bf16[16,2,128,128]{3,2,1,0:T(8,128)(2,1)S(1)}, u32[]{:S(2)}, u32[]{:S(2)}) async-start(bf16[16,2,128,128]{3,2,1,0:T(8,128)(2,1)} %prepare.2), calls=%async_computation | async-start | bytes 2097152 | tf_op jit(solution)/shard_map/all_to_all | solution.py:532
  12.6 17.0 %copy-start.5 = (f32[8,4096]{1,0:T(8,128)S(1)}, f32[8,4096]{1,0:T(8,128)}, u32[]{:S(2)}) copy-start(f32[8,4096]{1,0:T(8,128)} %mine.1) | copy-start | bytes 393220
  12.6 19.7 %copy-start.8 = (f32[128]{0:T(128)S(1)}, f32[128]{0:T(128)}, u32[]{:S(2)}) copy-start(f32[128]{0:T(128)} %param.10) | copy-start | bytes 1540
  25.9 25.8 %copy-start.2 = (bf16[16,2,128,128]{3,2,1,0:T(8,128)(2,1)}, bf16[16,2,128,128]{3,2,1,0:T(8,128)(2,1)S(1)}, u32[]{:S(2)}) copy-start(bf16[16,2,128,128]{3,2,1,0:T(8,128)(2,1)S(1)} %all-to-all-done.x) | copy-start | bytes 3145732
  25.9 33.8 %all-to-all-start.2 = ((bf16[16,2,128,128]{3,2,1,0:T(8,128)(2,1)}), bf16[16,2,128,128]{3,2,1,0:T(8,128)(2,1)S(1)}, u32[]{:S(2)}, u32[]{:S(2)}) async-start(bf16[16,2,128,128]{3,2,1,0:T(8,128)(2,1)} %prepare.3), calls=%async_computation.2 | async-start | bytes 2097152 | tf_op jit(solution)/shard_map/all_to_all | solution.py:532
  29.6 16.7 %collective-permute-start = (f32[8,4096]{1,0:T(8,128)S(1)}, f32[8,4096]{1,0:T(8,128)S(1)}, u32[]{:S(2)}, u32[]{:S(2)}) collective-permute-start(f32[8,4096]{1,0:T(8,128)S(1)} %copy-done.5), channel_id=1, source_target_pairs={{0,16},{1,17},{2,18},{3,19},{4,20},{5,21},{6,22},{7,23},{8,24},{9,... | collective-permute-start | bytes 393224 | tf_op jit(solution)/shard_map/ppermute | solution.py:542
  32.3 14.0 %collective-permute-start.1 = (f32[1,128]{1,0:T(1,128)S(1)}, f32[1,128]{1,0:T(1,128)S(1)}, u32[]{:S(2)}, u32[]{:S(2)}) collective-permute-start(f32[1,128]{1,0:T(1,128)S(1)} %bitcast.32), channel_id=1, source_target_pairs={{0,16},{1,17},{2,18},{3,19},{4,20},{5,21},{6,22},{7,23},{8,24},{9,... | collective-permute-start | bytes 1544 | tf_op jit(solution)/shard_map/ppermute | solution.py:542
  46.3 0.5 copy-start.9
  46.8 0.7 copy-start.6
  59.7 6.6 %copy-start.3 = (bf16[16,2,128,128]{3,2,1,0:T(8,128)(2,1)S(1)}, bf16[16,2,128,128]{3,2,1,0:T(8,128)(2,1)}, u32[]{:S(2)}) copy-start(bf16[16,2,128,128]{3,2,1,0:T(8,128)(2,1)} %copy-done.2) | copy-start | bytes 3145732
  59.8 7.6 %copy-start.4 = (bf16[16,2,128,128]{3,2,1,0:T(8,128)(2,1)}, bf16[16,2,128,128]{3,2,1,0:T(8,128)(2,1)S(1)}, u32[]{:S(2)}) copy-start(bf16[16,2,128,128]{3,2,1,0:T(8,128)(2,1)S(1)} %all-to-all-done.2.y) | copy-start | bytes 3145732
  59.8 72.1 %all-to-all-start.1 = ((bf16[16,2,128,128]{3,2,1,0:T(8,128)(2,1)}), bf16[16,2,128,128]{3,2,1,0:T(8,128)(2,1)S(1)}, u32[]{:S(2)}, u32[]{:S(2)}) async-start(bf16[16,2,128,128]{3,2,1,0:T(8,128)(2,1)} %shard_map.110), calls=%async_computation.1 | async-start | bytes 2097152 | tf_op jit(solution)/shard_map/all_to_all | solution.py:532
  67.4 38.4 %collective-permute-start.2 = (bf16[16,128,128]{2,1,0:T(8,128)(2,1)}, bf16[16,128,128]{2,1,0:T(8,128)(2,1)S(1)}, u32[]{:S(2)}, u32[]{:S(2)}) collective-permute-start(bf16[16,128,128]{2,1,0:T(8,128)(2,1)} %get-tuple-element.31), channel_id=1, source_target_pairs={{0,16},{1,17},{2,18},{3,19},{4,20},{5,21},{6,22},{7,23},{8,24},{9,... | collective-permute-start | bytes 1572872 | tf_op jit(solution)/shard_map/ppermute | solution.py:542
  68.2 48.3 %collective-permute-start.3 = (bf16[16,128,128]{2,1,0:T(8,128)(2,1)}, bf16[16,128,128]{2,1,0:T(8,128)(2,1)S(1)}, u32[]{:S(2)}, u32[]{:S(2)}) collective-permute-start(bf16[16,128,128]{2,1,0:T(8,128)(2,1)} %get-tuple-element.30), channel_id=1, source_target_pairs={{0,16},{1,17},{2,18},{3,19},{4,20},{5,21},{6,22},{7,23},{8,24},{9,... | collective-permute-start | bytes 1572872 | tf_op jit(solution)/shard_map/ppermute | solution.py:542
  105.8 10.7 %copy-start.10 = (bf16[16,128,128]{2,1,0:T(8,128)(2,1)}, bf16[16,128,128]{2,1,0:T(8,128)(2,1)S(1)}, u32[]{:S(2)}) copy-start(bf16[16,128,128]{2,1,0:T(8,128)(2,1)S(1)} %collective-permute-done.2.r_a) | copy-start | bytes 1572868
  116.5 0.8 copy-start.11
  131.8 14.8 %copy-start = (bf16[16,2,128,128]{3,2,1,0:T(8,128)(2,1)}, bf16[16,2,128,128]{3,2,1,0:T(8,128)(2,1)S(1)}, u32[]{:S(2)}) copy-start(bf16[16,2,128,128]{3,2,1,0:T(8,128)(2,1)S(1)} %all-to-all-done.1.one) | copy-start | bytes 3145732
  131.8 21.6 %all-to-all-start.3 = ((bf16[16,2,128,128]{3,2,1,0:T(8,128)(2,1)}), bf16[16,2,128,128]{3,2,1,0:T(8,128)(2,1)S(1)}, u32[]{:S(2)}, u32[]{:S(2)}) async-start(bf16[16,2,128,128]{3,2,1,0:T(8,128)(2,1)} %shard_map.112), calls=%async_computation.3 | async-start | bytes 2097152 | tf_op jit(solution)/shard_map/all_to_all | solution.py:532
  137.7 13.2 %collective-permute-start.4 = (f32[8,2176]{1,0:T(8,128)}, f32[8,2176]{1,0:T(8,128)S(1)}, u32[]{:S(2)}, u32[]{:S(2)}) collective-permute-start(f32[8,2176]{1,0:T(8,128)} %shard_map.114), channel_id=1, source_target_pairs={{0,16},{1,17},{2,18},{3,19},{4,20},{5,21},{6,22},{7,23},{8,24},{9,... | collective-permute-start | bytes 208904 | tf_op jit(solution)/shard_map/ppermute | solution.py:542
  150.9 0.6 copy-start.7
  153.4 1.0 copy-start.1
